TPU v7x, 32 devices: a whole 2x2x4 slice. The times are simulated.
32 devices in a mesh: dp: 4 (over y, x), ctx: 2 (over core), mp: 4 (over z).
Axes of the slice: x: 2, y: 2, z: 4, core: 2. Of those that a mesh axis runs over, the one named last changes fastest.
Arguments:
- inputs: bfloat16 [12, 1024, 1536], P('dp', ('ctx', 'mp')), may hold values from -6 to 6
- w_query: bfloat16 [1536, 1536], P(('dp', 'ctx'), 'mp'), may hold values from -0.21875 to 0.21875
- w_key: bfloat16 [1536, 1536], P(('dp', 'ctx'), 'mp'), may hold values from -0.21875 to 0.21875
- w_value: bfloat16 [1536, 1536], P(('dp', 'ctx'), 'mp'), may hold values from -0.15625 to 0.15625
- w_out: bfloat16 [1536, 1536], P('mp', ('dp', 'ctx')), may hold values from -0.875 to 0.875
- w_up: bfloat16 [1536, 8, 768], P(('dp', 'ctx'), None, 'mp'), may hold values from -0.15625 to 0.15625
- w_down: bfloat16 [8, 768, 1536], P(None, 'mp', ('dp', 'ctx')), may hold values from -0.15625 to 0.15625
- gain_attn: bfloat16 [1536], P(('dp', 'ctx')), may hold values from 0.099609375 to 1.8984375
- gain_ffn: bfloat16 [1536], P(('dp', 'ctx')), may hold values from 0.099609375 to 1.8984375
- cotangent: bfloat16 [12, 1024, 1536], P('dp', ('ctx', 'mp')), may hold values from -6 to 6
Outputs:
- outputs: bfloat16 [12, 1024, 1536], P('dp', ('ctx', 'mp'))
- input_grads: float32 [12, 1024, 1536], P('dp', ('ctx', 'mp'))
- grad_query: float32 [1536, 1536], P(('dp', 'ctx'), 'mp')
- grad_key: float32 [1536, 1536], P(('dp', 'ctx'), 'mp')
- grad_value: float32 [1536, 1536], P(('dp', 'ctx'), 'mp')
- grad_out: float32 [1536, 1536], P('mp', ('dp', 'ctx'))
- grad_up: float32 [1536, 8, 768], P(('dp', 'ctx'), None, 'mp')
- grad_down: float32 [8, 768, 1536], P(None, 'mp', ('dp', 'ctx'))
- grad_gain_attn: float32 [1536], P(('dp', 'ctx'))
- grad_gain_ffn: float32 [1536], P(('dp', 'ctx'))
All inputs are finite; a program needn't handle non-finite values.
Results may differ from a plain program's by a relative error of at most 0.015.
Values may be sent and summed in bfloat16 or wider, within the bound.
No kernel may reach another device: no remote copies, remote signals or barrier semaphores. Data moves between devices by JAX's collectives and lax.ppermute only.
A program may use at most 256 MiB of HBM per device.

v0:
```python
import jax
import jax.numpy as jnp
from jax import lax
from jax.sharding import PartitionSpec as P

HEAD = 128
EPSILON = 1e-06
NEGATIVE = -1e30


def from_behind(shard, axis, by):
    devices = lax.axis_size(axis)
    pairs = [(i, i + by) for i in range(devices) if 0 <= i + by < devices]
    return lax.ppermute(shard, axis, pairs)


def normalize(values, gain_vec):
    inv_rms = lax.rsqrt(jnp.mean(values * values, axis=-1, keepdims=True) + EPSILON)
    return values * inv_rms * gain_vec


def unit_rows(values):
    return values * lax.rsqrt(jnp.mean(values * values, axis=-1, keepdims=True) + EPSILON)


def norm_back(values, gain_vec, grad_normed):
    inv_rms = lax.rsqrt(jnp.mean(values * values, axis=-1, keepdims=True) + EPSILON)
    weighted = grad_normed * gain_vec
    return inv_rms * weighted - values * (inv_rms * inv_rms * inv_rms) * jnp.mean(
        weighted * values, axis=-1, keepdims=True
    )


def rotation(positions, head_size):
    half_size = head_size // 2
    frequency = 10000.0 ** (-jnp.arange(half_size, dtype=jnp.float32) / half_size)
    angles = positions.astype(jnp.float32)[:, None] * frequency[None, :]
    return (jnp.cos(angles)[:, None, :], jnp.sin(angles)[:, None, :])


def rotate(values, cosine, sine_part):
    half_size = values.shape[-1] // 2
    leading = values[..., :half_size]
    trailing = values[..., half_size:]
    return jnp.concatenate(
        [leading * cosine - trailing * sine_part, trailing * cosine + leading * sine_part], axis=-1
    )


def gelu_tanh(values):
    return jax.nn.gelu(values, approximate=True)


def local(inputs, w_query, w_key, w_value, w_out, w_up, w_down, gain_attn, gain_ffn, cotangent):
    query_full, key_full, value_full, out_full, up_full, down_full, gain_a_low, gain_f_low = (
        lax.all_gather(w_query, ("dp", "ctx"), axis=0, tiled=True),
        lax.all_gather(w_key, ("dp", "ctx"), axis=0, tiled=True),
        lax.all_gather(w_value, ("dp", "ctx"), axis=0, tiled=True),
        lax.all_gather(w_out, ("dp", "ctx"), axis=1, tiled=True),
        lax.all_gather(w_up, ("dp", "ctx"), axis=0, tiled=True),
        lax.all_gather(w_down, ("dp", "ctx"), axis=2, tiled=True),
        lax.all_gather(gain_attn, ("dp", "ctx"), axis=0, tiled=True),
        lax.all_gather(gain_ffn, ("dp", "ctx"), axis=0, tiled=True),
    )
    gain_first = gain_a_low.astype(jnp.float32)
    gain_second = gain_f_low.astype(jnp.float32)
    inputs_all, cotangent_all = (
        lax.all_gather(inputs, "mp", axis=1, tiled=True),
        lax.all_gather(cotangent, "mp", axis=1, tiled=True),
    )
    count = inputs_all.shape[0]
    length_half = inputs_all.shape[1]
    width = inputs_all.shape[2]
    shard_len = inputs.shape[1]
    total_rows = count * length_half
    mp_count = lax.axis_size("mp")
    mp_index = lax.axis_index("mp")
    ctx_index = lax.axis_index("ctx")
    head_count = query_full.shape[1] // HEAD
    factor = HEAD ** (-0.5)
    positions = ctx_index * length_half + jnp.arange(length_half, dtype=jnp.int32)
    cosine, sine_part = rotation(positions, HEAD)
    inputs_f = inputs_all.astype(jnp.float32)
    flat_first = normalize(inputs_f, gain_first).astype(jnp.bfloat16).reshape(total_rows, width)

    def project(matrix):
        return jnp.dot(flat_first, matrix, preferred_element_type=jnp.float32).reshape(
            count, length_half, head_count, HEAD
        )

    query_rows = rotate(project(query_full), cosine, sine_part).astype(jnp.bfloat16)
    key_rows = rotate(project(key_full), cosine, sine_part).astype(jnp.bfloat16)
    value_rows = project(value_full).astype(jnp.bfloat16)
    early_keys, early_values = from_behind((key_rows, value_rows), "ctx", 1)
    row_ids = jnp.arange(length_half)[:, None]
    col_ids = jnp.arange(2 * length_half)[None, :]
    visible = jnp.where(col_ids < length_half, ctx_index >= 1, col_ids - length_half <= row_ids)

    def scores_of(query_one, keys_all):
        raw_scores = (
            jnp.einsum("qhd,khd->hqk", query_one, keys_all, preferred_element_type=jnp.float32)
            * factor
        )
        return jnp.where(visible[None], raw_scores, NEGATIVE)

    def attend(package):
        query_one, key_one, value_one, key_early, value_early = package
        keys_all = jnp.concatenate([key_early, key_one], 0)
        values_all = jnp.concatenate([value_early, value_one], 0)
        scores = scores_of(query_one, keys_all)
        largest = jnp.max(scores, axis=-1, keepdims=True)
        exponent = jnp.exp(scores - largest)
        totals = jnp.sum(exponent, axis=-1, keepdims=True)
        softened = exponent / totals
        mixed_one = jnp.einsum(
            "hqk,khd->qhd",
            softened.astype(jnp.bfloat16),
            values_all,
            preferred_element_type=jnp.float32,
        )
        return (mixed_one.astype(jnp.bfloat16), (largest + jnp.log(totals))[..., 0])

    mixed_rows, log_totals = lax.map(
        attend, (query_rows, key_rows, value_rows, early_keys, early_values)
    )
    mixed_flat = mixed_rows.reshape(total_rows, head_count * HEAD)
    attended = lax.psum(jnp.dot(mixed_flat, out_full, preferred_element_type=jnp.float32), "mp")
    hidden_state = inputs_f + attended.reshape(count, length_half, width)
    normed_second = (
        normalize(hidden_state, gain_second).astype(jnp.bfloat16).reshape(total_rows, width)
    )
    cot_flat = cotangent_all.reshape(total_rows, width)
    block_width = up_full.shape[2]
    block_total = up_full.shape[1]

    def ffn_both(rows, grad_rows, blocks):
        used = blocks * block_width
        up_part = up_full[:, :blocks].reshape(width, used)
        down_part = down_full[:blocks].reshape(used, width)
        upped = jnp.dot(rows, up_part, preferred_element_type=jnp.float32)
        activated, gelu_pull = jax.vjp(gelu_tanh, upped)
        activated_low = activated.astype(jnp.bfloat16)
        result = jnp.dot(activated_low, down_part, preferred_element_type=jnp.float32)
        grad_act = jnp.einsum("rd,wd->rw", grad_rows, down_part, preferred_element_type=jnp.float32)
        grad_upped = gelu_pull(grad_act)[0].astype(jnp.bfloat16)
        grad_down_part = jnp.einsum(
            "rw,rd->wd", activated_low, grad_rows, preferred_element_type=jnp.float32
        )
        grad_up_part = jnp.einsum("rd,rw->dw", rows, grad_upped, preferred_element_type=jnp.float32)
        grad_in = jnp.einsum("rw,dw->rd", grad_upped, up_part, preferred_element_type=jnp.float32)
        grad_up_pad = jnp.pad(
            grad_up_part.reshape(width, blocks, block_width),
            ((0, 0), (0, block_total - blocks), (0, 0)),
        )
        grad_down_pad = jnp.pad(
            grad_down_part.reshape(blocks, block_width, width),
            ((0, block_total - blocks), (0, 0), (0, 0)),
        )
        return (result, grad_in, grad_up_pad, grad_down_pad)

    def make_branch(blocks):

        def branch_run(rows, grad_rows):
            return ffn_both(rows, grad_rows, blocks)

        return branch_run

    grain = lax.axis_index("dp") % 4
    ffn_part, grad_second_part, grad_up_sum, grad_down_sum = lax.switch(
        grain, [make_branch(2**grain_level) for grain_level in range(4)], normed_second, cot_flat
    )
    grad_second_part = grad_second_part.reshape(count, length_half, width)
    gain_second_part = jnp.sum(grad_second_part * unit_rows(hidden_state), axis=(0, 1))
    ffn_shard, grad_second_shard, gain_second_sum = (
        lax.psum_scatter(
            ffn_part.reshape(count, length_half, width), "mp", scatter_dimension=1, tiled=True
        ),
        lax.psum_scatter(grad_second_part, "mp", scatter_dimension=1, tiled=True),
        lax.psum_scatter(
            jnp.broadcast_to(gain_second_part, (mp_count, width)),
            "mp",
            scatter_dimension=0,
            tiled=True,
        ),
    )
    gain_second_grad = gain_second_sum[0]
    hidden_shard = lax.dynamic_slice_in_dim(hidden_state, mp_index * shard_len, shard_len, 1)
    outputs = (hidden_shard + ffn_shard).astype(jnp.bfloat16)
    grad_hidden_shard = cotangent.astype(jnp.float32) + norm_back(
        hidden_shard, gain_second, grad_second_shard
    )
    grad_hidden_low = lax.all_gather(
        grad_hidden_shard.astype(jnp.bfloat16), "mp", axis=1, tiled=True
    ).reshape(total_rows, width)
    grad_out_w = jnp.einsum(
        "rc,rd->cd", mixed_flat, grad_hidden_low, preferred_element_type=jnp.float32
    )
    grad_mixed = jnp.einsum(
        "rd,cd->rc", grad_hidden_low, out_full, preferred_element_type=jnp.float32
    )
    grad_mixed = grad_mixed.astype(jnp.bfloat16).reshape(count, length_half, head_count, HEAD)

    def attend_back(package):
        query_one, key_one, value_one, key_early, value_early, log_one, grad_one = package
        keys_all = jnp.concatenate([key_early, key_one], 0)
        values_all = jnp.concatenate([value_early, value_one], 0)
        scores = scores_of(query_one, keys_all)
        softened = jnp.exp(scores - log_one[..., None])
        grad_soft = jnp.einsum(
            "qhd,khd->hqk", grad_one, values_all, preferred_element_type=jnp.float32
        )
        grad_values = jnp.einsum(
            "hqk,qhd->khd",
            softened.astype(jnp.bfloat16),
            grad_one,
            preferred_element_type=jnp.float32,
        )
        inner = jnp.sum(grad_soft * softened, axis=-1, keepdims=True)
        grad_scores = (softened * (grad_soft - inner)).astype(jnp.bfloat16)
        grad_queries = (
            jnp.einsum("hqk,khd->qhd", grad_scores, keys_all, preferred_element_type=jnp.float32)
            * factor
        )
        grad_keys = (
            jnp.einsum("hqk,qhd->khd", grad_scores, query_one, preferred_element_type=jnp.float32)
            * factor
        )
        return (
            grad_queries,
            grad_keys[length_half:],
            grad_keys[:length_half],
            grad_values[length_half:],
            grad_values[:length_half],
        )

    grad_queries, grad_key_own, grad_key_early, grad_value_own, grad_value_early = lax.map(
        attend_back,
        (query_rows, key_rows, value_rows, early_keys, early_values, log_totals, grad_mixed),
    )
    key_back, value_back = (
        from_behind(grad_key_early.astype(jnp.bfloat16), "ctx", -1).astype(grad_key_early.dtype),
        from_behind(grad_value_early.astype(jnp.bfloat16), "ctx", -1).astype(
            grad_value_early.dtype
        ),
    )
    grad_query_low = (
        rotate(grad_queries, cosine, -sine_part).astype(jnp.bfloat16).reshape(total_rows, -1)
    )
    grad_key_low = (
        rotate(grad_key_own + key_back, cosine, -sine_part)
        .astype(jnp.bfloat16)
        .reshape(total_rows, -1)
    )
    grad_value_low = (grad_value_own + value_back).astype(jnp.bfloat16).reshape(total_rows, -1)
    grad_query_w = jnp.einsum(
        "rd,rc->dc", flat_first, grad_query_low, preferred_element_type=jnp.float32
    )
    grad_key_w = jnp.einsum(
        "rd,rc->dc", flat_first, grad_key_low, preferred_element_type=jnp.float32
    )
    grad_value_w = jnp.einsum(
        "rd,rc->dc", flat_first, grad_value_low, preferred_element_type=jnp.float32
    )
    grad_first_part = jnp.einsum(
        "rc,dc->rd", grad_query_low, query_full, preferred_element_type=jnp.float32
    )
    grad_first_part = grad_first_part + jnp.einsum(
        "rc,dc->rd", grad_key_low, key_full, preferred_element_type=jnp.float32
    )
    grad_first_part = grad_first_part + jnp.einsum(
        "rc,dc->rd", grad_value_low, value_full, preferred_element_type=jnp.float32
    )
    grad_first_part = grad_first_part.reshape(count, length_half, width)
    gain_first_part = jnp.sum(grad_first_part * unit_rows(inputs_f), axis=(0, 1))
    grad_first_shard, gain_first_sum = (
        lax.psum_scatter(
            grad_first_part.astype(jnp.bfloat16), "mp", scatter_dimension=1, tiled=True
        ).astype(jnp.float32),
        lax.psum_scatter(
            jnp.broadcast_to(gain_first_part, (mp_count, width)).astype(jnp.bfloat16),
            "mp",
            scatter_dimension=0,
            tiled=True,
        ).astype(jnp.float32),
    )
    input_grads = grad_hidden_shard + norm_back(
        inputs.astype(jnp.float32), gain_first, grad_first_shard
    )
    (
        grad_query_out,
        grad_key_out,
        grad_value_out,
        grad_out_out,
        grad_up_out,
        grad_down_out,
        gain_attn_out,
        gain_ffn_out,
    ) = (
        lax.psum_scatter(grad_query_w, ("dp", "ctx"), scatter_dimension=0, tiled=True),
        lax.psum_scatter(grad_key_w, ("dp", "ctx"), scatter_dimension=0, tiled=True),
        lax.psum_scatter(grad_value_w, ("dp", "ctx"), scatter_dimension=0, tiled=True),
        lax.psum_scatter(grad_out_w, ("dp", "ctx"), scatter_dimension=1, tiled=True),
        lax.psum_scatter(grad_up_sum, ("dp", "ctx"), scatter_dimension=0, tiled=True),
        lax.psum_scatter(grad_down_sum, ("dp", "ctx"), scatter_dimension=2, tiled=True),
        lax.psum_scatter(gain_first_sum[0], ("dp", "ctx"), scatter_dimension=0, tiled=True),
        lax.psum_scatter(gain_second_grad, ("dp", "ctx"), scatter_dimension=0, tiled=True),
    )
    return (
        outputs,
        input_grads,
        grad_query_out,
        grad_key_out,
        grad_value_out,
        grad_out_out,
        grad_up_out,
        grad_down_out,
        gain_attn_out,
        gain_ffn_out,
    )


def solution(mesh):
    in_specs = (
        P("dp", ("ctx", "mp"), None),
        P(("dp", "ctx"), "mp"),
        P(("dp", "ctx"), "mp"),
        P(("dp", "ctx"), "mp"),
        P("mp", ("dp", "ctx")),
        P(("dp", "ctx"), None, "mp"),
        P(None, "mp", ("dp", "ctx")),
        P(("dp", "ctx")),
        P(("dp", "ctx")),
        P("dp", ("ctx", "mp"), None),
    )
    out_specs = (
        P("dp", ("ctx", "mp"), None),
        P("dp", ("ctx", "mp"), None),
        P(("dp", "ctx"), "mp"),
        P(("dp", "ctx"), "mp"),
        P(("dp", "ctx"), "mp"),
        P("mp", ("dp", "ctx")),
        P(("dp", "ctx"), None, "mp"),
        P(None, "mp", ("dp", "ctx")),
        P(("dp", "ctx")),
        P(("dp", "ctx")),
    )
    return jax.shard_map(local, mesh=mesh, in_specs=in_specs, out_specs=out_specs, check_vma=False)
```

profile of v0, /device:TPU:0, one launch (start us, length us, event | category | flops | bytes accessed | tf_op | source)
XLA Modules:
  0.0 1783.2 jit_solution(12301022891588044339)
XLA Ops:
  13.7 15.5 all-reduce.13
  38.4 24.4 %all-gather.14.cloned.1.call-done = bf16[1536,384]{1,0:T(8,128)(2,1)} async-done(((bf16[192,384]{1,0:T(8,128)(2,1)}), bf16[1536,384]{1,0:T(8,128)(2,1)}) %all-gather.14.cloned.1.call-update) | async-done | bytes 1179664 | tf_op jit(solution)/shard_map/all_gather | solution.py:56
  64.4 24.4 %all-gather.12.cloned.1.call-done = bf16[1536,384]{1,0:T(8,128)(2,1)} async-done(((bf16[192,384]{1,0:T(8,128)(2,1)}), bf16[1536,384]{1,0:T(8,128)(2,1)}) %all-gather.12.cloned.1.call-update) | async-done | bytes 1179664 | tf_op jit(solution)/shard_map/all_gather | solution.py:58
  91.2 88.5 %all-gather.10.cloned.1.call-done = bf16[3,512,1536]{2,1,0:T(8,128)(2,1)} async-done(((bf16[3,128,1536]{2,1,0:T(8,128)(2,1)}), bf16[3,512,1536]{2,1,0:T(8,128)(2,1)}) %all-gather.10.cloned.1.call-update) | async-done | bytes 4718608 | tf_op jit(solution)/shard_map/all_gather | solution.py:68
  207.8 42.8 %while.32 = (s32[]{:T(128)}, bf16[3,512,3,128]{1,3,2,0:T(8,128)(2,1)}, f32[3,3,512]{2,1,0:T(4,128)}, bf16[3,512,3,128]{3,1,2,0:T(8,128)(2,1)}, bf16[3,512,3,128]...) while((s32[]{:T(128)}, ...), condition=%wide.region_4.5_spmd.clone, body=%wide.region_1.4_spmd.clone.sunk | while | flops 828570112 | bytes 53273240 | solution.py:123
  254.4 8.0 fusion.133
  266.0 319.7 %all-reduce.16.cloned.1.call-done = f32[3,512,1536]{2,1,0:T(8,128)} async-done(((f32[3,512,1536]{2,1,0:T(8,128)}), f32[3,512,1536]{2,1,0:T(8,128)}) %all-reduce.16.cloned.1.call-update) | async-done | bytes 9437200 | tf_op jit(solution)/shard_map/psum | solution.py:127
  585.7 10.6 multiply_reduce_fusion.2
  596.9 6.7 multiply_convert_fusion.13
  603.6 72.0 %all-gather.24.cloned.1.call-done = bf16[3,512,1536]{2,1,0:T(8,128)(2,1)} async-done(((bf16[3,128,1536]{2,1,0:T(8,128)(2,1)}), bf16[3,512,1536]{2,1,0:T(8,128)(2,1)}) %all-gather.24.cloned.1.call-update) | async-done | bytes 4718608 | tf_op jit(solution)/shard_map/all_gather | solution.py:69
  675.7 46.5 %all-gather.22.cloned.1.call-done = bf16[8,192,1536]{1,0,2:T(8,128)(2,1)} async-done(((bf16[8,192,192]{1,0,2:T(8,128)(2,1)}), bf16[8,192,1536]{1,0,2:T(8,128)(2,1)}) %all-gather.22.cloned.1.call-update) | async-done | bytes 4718608 | tf_op jit(solution)/shard_map/all_gather | solution.py:61
  722.1 47.4 %all-gather.20.cloned.1.call-done = bf16[1536,8,192]{2,1,0:T(8,128)(2,1)} async-done(((bf16[192,8,192]{2,1,0:T(8,128)(2,1)}), bf16[1536,8,192]{2,1,0:T(8,128)(2,1)}) %all-gather.20.cloned.1.call-update) | async-done | bytes 4718608 | tf_op jit(solution)/shard_map/all_gather | solution.py:60
  769.6 72.1 %conditional.1 = (f32[1536,1536]{1,0:T(8,128)}, f32[1536,1536]{1,0:T(8,128)}, f32[1536,8,192]{0,2,1:T(8,128)}, f32[8,192,1536]{2,1,0:T(8,128)}) conditional(s32[]{:T(128)} %clamp.3, (bf16[1536,8,192]{2,1,0:T(8,128)(2,1)}, bf16[1536,1536]{1,0:T(8,128)(2,1)}, bf16[8,192,1536]{1,0,2:T(8,128)(2,1)}, ...), branch_computations={%region_7.8_spmd, %region_8.9_spmd, %region_9.10_spmd, %region_10.... | conditional | flops 43576197120 | bytes 273678624 | solution.py:169
  769.7 8.8 copy.70
  782.7 8.8 copy.71
  841.8 204.0 %reduce-scatter.14.cloned.1.call-done = f32[3,128,1536]{2,1,0:T(8,128)} async-done(((f32[3,512,1536]{2,1,0:T(8,128)}), f32[3,128,1536]{2,1,0:T(8,128)}) %reduce-scatter.14.cloned.1.call-update) | async-done | bytes 2359312 | tf_op jit(solution)/shard_map/reduce_scatter | solution.py:178
  1052.9 12.9 copy.90
  1065.8 13.1 reshape.343
  1079.0 64.2 %all-gather.26.cloned.1.call-done = bf16[3,512,1536]{2,1,0:T(8,128)(2,1)} async-done(((bf16[3,128,1536]{2,1,0:T(8,128)(2,1)}), bf16[3,512,1536]{2,1,0:T(8,128)(2,1)}) %all-gather.26.cloned.1.call-update) | async-done | bytes 4718608 | tf_op jit(solution)/shard_map/all_gather | solution.py:192
  1151.9 52.4 %while.33 = (s32[]{:T(128)}, f32[3,512,3,128]{1,3,2,0:T(8,128)}, f32[3,512,3,128]{1,3,2,0:T(8,128)}, bf16[3,512,3,128]{1,3,2,0:T(8,128)(2,1)}, f32[3,512,3,128]{...) while((s32[]{:T(128)}, f32[3,512,3,128]{1,3,2,0:T(8,128)}, ...), condition=%wide.region_18.19_spmd.clone, body=%wide.region_16.18_spmd.clone.sunk | while | flops 2043214336 | bytes 65065664 | solution.py:236
  1244.9 12.9 copy.85
  1258.3 6.9 fusion.131
  1288.0 7.4 multiply_reduce_fusion.1
  1295.4 19.1 %all-reduce.10 = f32[4,1536]{1,0:T(4,128)S(1)} all-reduce(f32[4,1536]{1,0:T(4,128)S(1)} %broadcast_in_dim.98), channel_id=13, replica_groups=mesh['dp'=4,'ctx'=2,'mp'=4] {'mp'}, use_global_device_ids=true, to_apply=%region_31.32.clone | all-reduce | flops 6144 | bytes 49152
  1326.6 17.4 all-reduce.8
  1345.9 23.9 %all-reduce.12 = (f32[1536]{0:T(1024)}, f32[1536]{0:T(1024)}) all-reduce(f32[1536]{0:T(1024)} %fusion.144, f32[1536]{0:T(1024)} %dynamic-slice_reduce_fusion), channel_id=12, replica_groups=mesh['dp'=4,'ctx'=2,'mp'=4] {'dp','ctx'}, use_global_device_ids=true, to_apply=%region_29.30.clone | all-reduce | flops 3072 | bytes 24576
  1375.5 117.7 %reduce-scatter.12.cloned.1.call-done = f32[3,128,1536]{2,1,0:T(8,128)} async-done(((f32[3,512,1536]{2,1,0:T(8,128)}), f32[3,128,1536]{2,1,0:T(8,128)}) %reduce-scatter.12.cloned.1.call-update) | async-done | bytes 2359312 | tf_op jit(solution)/shard_map/reduce_scatter | solution.py:175
  1498.3 92.1 %reduce-scatter.26.cloned.1.call-done = f32[192,8,192]{2,1,0:T(8,128)} async-done(((f32[1536,8,192]{2,1,0:T(8,128)}), f32[192,8,192]{2,1,0:T(8,128)}) %reduce-scatter.26.cloned.1.call-update) | async-done | bytes 1179664 | tf_op jit(solution)/shard_map/reduce_scatter | solution.py:303
  1590.4 46.3 %reduce-scatter.24.cloned.1.call-done = f32[384,192]{0,1:T(8,128)} async-done(((f32[384,1536]{0,1:T(8,128)}), f32[384,192]{0,1:T(8,128)}) %reduce-scatter.24.cloned.1.call-update) | async-done | bytes 294928 | tf_op jit(solution)/shard_map/reduce_scatter | solution.py:302
  1636.7 46.6 %reduce-scatter.22.cloned.1.call-done = f32[192,384]{1,0:T(8,128)} async-done(((f32[1536,384]{1,0:T(8,128)}), f32[192,384]{1,0:T(8,128)}) %reduce-scatter.22.cloned.1.call-update) | async-done | bytes 294928 | tf_op jit(solution)/shard_map/reduce_scatter | solution.py:301
  1683.4 46.3 %reduce-scatter.20.cloned.1.call-done = f32[192,384]{1,0:T(8,128)} async-done(((f32[1536,384]{1,0:T(8,128)}), f32[192,384]{1,0:T(8,128)}) %reduce-scatter.20.cloned.1.call-update) | async-done | bytes 294928 | tf_op jit(solution)/shard_map/reduce_scatter | solution.py:300
  1729.7 46.8 %reduce-scatter.18.cloned.1.call-done = f32[192,384]{1,0:T(8,128)} async-done(((f32[1536,384]{1,0:T(8,128)}), f32[192,384]{1,0:T(8,128)}) %reduce-scatter.18.cloned.1.call-update) | async-done | bytes 294928 | tf_op jit(solution)/shard_map/reduce_scatter | solution.py:299
  (285 shorter events, 286.3 us)
Async XLA Ops:
  7.2 29.7 %all-gather.16.cloned.1.call-start = ((), (), s32[]{:S(2)}) async-start(), calls=%async_computation.12 | async-start | bytes 1327104 | tf_op jit(solution)/shard_map/all_gather | solution.py:57
  7.9 54.9 %all-gather.14.cloned.1.call-start = ((), (), s32[]{:S(2)}) async-start(), calls=%async_computation.11 | async-start | bytes 1327104 | tf_op jit(solution)/shard_map/all_gather | solution.py:56
  8.7 80.2 %all-gather.12.cloned.1.call-start = ((), (), s32[]{:S(2)}) async-start(), calls=%async_computation.10 | async-start | bytes 1327104 | tf_op jit(solution)/shard_map/all_gather | solution.py:58
  9.4 170.3 %all-gather.10.cloned.1.call-start = ((), (), s32[]{:S(2)}) async-start(), calls=%async_computation.9 | async-start | bytes 5898240 | tf_op jit(solution)/shard_map/all_gather | solution.py:68
  10.0 244.5 %all-gather.18.cloned.1.call-start = ((), (), s32[]{:S(2)}) async-start(), calls=%async_computation.13 | async-start | bytes 1327104 | tf_op jit(solution)/shard_map/all_gather | solution.py:59
  29.3 153.9 %copy-start.25 = (f32[1536]{0:T(1024)}, f32[1536]{0:T(1024)S(1)}, u32[]{:S(2)}) copy-start(f32[1536]{0:T(1024)S(1)} %convert_element_type.148) | copy-start | bytes 18436
  30.5 158.2 %copy-start.14 = (f32[512,64]{0,1:T(8,128)}, f32[512,64]{0,1:T(8,128)S(1)}, u32[]{:S(2)}) copy-start(f32[512,64]{0,1:T(8,128)S(1)} %get-tuple-element.456) | copy-start | bytes 393220
  190.4 14.9 collective-permute-start.1
  197.0 10.7 collective-permute-start
  199.4 386.2 %all-reduce.16.cloned.1.call-start = ((), (), s32[]{:S(2)}) async-start(), calls=%async_computation.14 | async-start | bytes 18874368 | tf_op jit(solution)/shard_map/psum | solution.py:127
  262.5 413.2 %all-gather.24.cloned.1.call-start = ((), (), s32[]{:S(2)}) async-start(), calls=%async_computation.17 | async-start | bytes 5898240 | tf_op jit(solution)/shard_map/all_gather | solution.py:69
  263.2 458.9 %all-gather.22.cloned.1.call-start = ((), (), s32[]{:S(2)}) async-start(), calls=%async_computation.16 | async-start | bytes 7077888 | tf_op jit(solution)/shard_map/all_gather | solution.py:61
  265.1 504.4 %all-gather.20.cloned.1.call-start = ((), (), s32[]{:S(2)}) async-start(), calls=%async_computation.15 | async-start | bytes 7077888 | tf_op jit(solution)/shard_map/all_gather | solution.py:60
  265.9 779.9 %reduce-scatter.14.cloned.1.call-start = ((), (), s32[]{:S(2)}) async-start(), calls=%async_computation.19 | async-start | bytes 11796480 | tf_op jit(solution)/shard_map/reduce_scatter | solution.py:178
  265.9 330.4 %copy-start.22 = (f32[1536]{0:T(1024)}, f32[1536]{0:T(1024)S(1)}, u32[]{:S(2)}) copy-start(f32[1536]{0:T(1024)S(1)} %convert_element_type.152) | copy-start | bytes 18436
  841.7 204.1 %copy-start.23 = (f32[1536]{0:T(1024)S(1)}, f32[1536]{0:T(1024)}, u32[]{:S(2)}) copy-start(f32[1536]{0:T(1024)} %copy-done.22) | copy-start | bytes 18436
  841.7 301.5 %all-gather.26.cloned.1.call-start = ((), (), s32[]{:S(2)}) async-start(), calls=%async_computation.20 | async-start | bytes 5898240 | tf_op jit(solution)/shard_map/all_gather | solution.py:192
  841.7 207.7 %copy-start.8 = (bf16[3,128,1536]{2,1,0:T(8,128)(2,1)S(1)}, bf16[3,128,1536]{2,1,0:T(8,128)(2,1)}, u32[]{:S(2)}) copy-start(bf16[3,128,1536]{2,1,0:T(8,128)(2,1)} %param.27) | copy-start | bytes 3538948
  1052.8 262.9 %reduce-scatter.28.cloned.1.call-start = ((), (), s32[]{:S(2)}) async-start(), calls=%async_computation.27 | async-start | bytes 10616832
  1078.9 64.3 %copy-start.16 = (bf16[384,1536]{0,1:T(8,128)(2,1)S(1)}, bf16[384,1536]{0,1:T(8,128)(2,1)}, u32[]{:S(2)}) copy-start(bf16[384,1536]{0,1:T(8,128)(2,1)} %all-gather.18.cloned.1.call-done) | copy-start | bytes 3538948
  1079.0 293.5 %reduce-scatter.16.cloned.1.call-start = ((), (), s32[]{:S(2)}) async-start(), calls=%async_computation.21 | async-start | bytes 5898240 | tf_op jit(solution)/shard_map/reduce_scatter | solution.py:276
  1204.3 4.7 collective-permute-start.3
  1205.6 6.6 collective-permute-start.2
  1244.2 249.0 %reduce-scatter.12.cloned.1.call-start = ((), (), s32[]{:S(2)}) async-start(), calls=%async_computation.18 | async-start | bytes 11796480 | tf_op jit(solution)/shard_map/reduce_scatter | solution.py:175
  1244.8 345.6 %reduce-scatter.26.cloned.1.call-start = ((), (), s32[]{:S(2)}) async-start(), calls=%async_computation.26 | async-start | bytes 14155776 | tf_op jit(solution)/shard_map/reduce_scatter | solution.py:303
  1257.8 378.9 %reduce-scatter.24.cloned.1.call-start = ((), (), s32[]{:S(2)}) async-start(), calls=%async_computation.25 | async-start | bytes 2654208 | tf_op jit(solution)/shard_map/reduce_scatter | solution.py:302
  1265.2 418.1 %reduce-scatter.22.cloned.1.call-start = ((), (), s32[]{:S(2)}) async-start(), calls=%async_computation.24 | async-start | bytes 2654208 | tf_op jit(solution)/shard_map/reduce_scatter | solution.py:301
  1271.7 457.9 %reduce-scatter.20.cloned.1.call-start = ((), (), s32[]{:S(2)}) async-start(), calls=%async_computation.23 | async-start | bytes 2654208 | tf_op jit(solution)/shard_map/reduce_scatter | solution.py:300
  1278.2 498.2 %reduce-scatter.18.cloned.1.call-start = ((), (), s32[]{:S(2)}) async-start(), calls=%async_computation.22 | async-start | bytes 2654208 | tf_op jit(solution)/shard_map/reduce_scatter | solution.py:299
  1319.4 53.1 %copy-start.26 = (f32[1536]{0:T(1024)S(1)}, f32[1536]{0:T(1024)}, u32[]{:S(2)}) copy-start(f32[1536]{0:T(1024)} %copy-done.25) | copy-start | bytes 18436
  1326.0 167.3 %copy-start.6 = (f32[3,128,1536]{2,1,0:T(8,128)S(1)}, f32[3,128,1536]{2,1,0:T(8,128)}, u32[]{:S(2)}) copy-start(f32[3,128,1536]{2,1,0:T(8,128)} %reduce-scatter.14.cloned.1.call-done) | copy-start | bytes 7077892
  1326.0 167.2 %copy-start.24 = (f32[1536]{0:T(1024)S(1)}, f32[1536]{0:T(1024)}, u32[]{:S(2)}) copy-start(f32[1536]{0:T(1024)} %copy-done.22) | copy-start | bytes 18436
  (33 other events, 202.7 us)
Sparse Core Ops, SparseCore 0:
  9.9 26.9 all-gather.15
  38.8 24.0 all-gather.13
  64.7 24.0 all-gather.11
  90.3 89.3 all-gather.9
  199.5 22.5 all-gather.17
  262.6 323.0 all-reduce.15
  587.2 88.3 all-gather.23
  678.1 43.9 all-gather.21
  724.0 45.5 all-gather.19
  841.8 203.9 reduce-scatter.13
  1052.9 90.2 all-gather.25
  1146.6 74.9 reduce-scatter.27
  1244.4 84.7 reduce-scatter.15
  1331.3 161.8 reduce-scatter.11
  1497.1 93.2 reduce-scatter.25
  1594.2 42.4 reduce-scatter.23
  1640.9 42.4 reduce-scatter.21
  1687.1 42.4 reduce-scatter.19
  1734.0 42.4 reduce-scatter.17
where the time goes:
time: 1790 us; the launch traced here: 1780 us
  waiting for transfers between devices  1300 us (73%)
  local copies, waits for them, and re-layouts  144 us (8%)
  matrix products  128 us (7%)
  other arithmetic  87.2 us (5%)
  blocking collectives  75.9 us (4%)
  loops' own time  21.7 us (1%)
    psum x1, waiting for transfers between devices, local(): lax.psum(jnp.dot(mixed_flat, out_full, preferred_element_type=jnp.float32...  320 us
    reduce_scatter x1, waiting for transfers between devices, local(): lax.psum_scatter(grad_second_part, 'mp', scatter_dimension=1, tiled=True)  204 us
    reduce_scatter x1, waiting for transfers between devices, local(): lax.psum_scatter(ffn_part.reshape(count, length_half, width), 'mp', scatt...  118 us
    reduce_scatter x1, waiting for transfers between devices, local(): lax.psum_scatter(grad_up_sum, ('dp', 'ctx'), scatter_dimension=0, tiled=T...  92.1 us
    all_gather x1, waiting for transfers between devices, local(): lax.all_gather(inputs, 'mp', axis=1, tiled=True)  88.5 us
    unnamed x4, blocking collectives  75.9 us
    all_gather x1, waiting for transfers between devices, local(): lax.all_gather(cotangent, 'mp', axis=1, tiled=True)  72 us
    all_gather x1, waiting for transfers between devices, local(): lax.all_gather(grad_hidden_shard.astype(jnp.bfloat16), 'mp', axis=1, tile...  64.2 us
  transfers between devices with their start and end apart: 23, of which 17 were waited for; matrix products, arithmetic and copies ran while one was open for 15% of the time, Pallas kernels for 0%

commit v1 on v0

--- a/solution.py
+++ b/solution.py
@@ -124,7 +124,9 @@
         attend, (query_rows, key_rows, value_rows, early_keys, early_values)
     )
     mixed_flat = mixed_rows.reshape(total_rows, head_count * HEAD)
-    attended = lax.psum(jnp.dot(mixed_flat, out_full, preferred_element_type=jnp.float32), "mp")
+    block = jnp.dot(mixed_flat, out_full, preferred_element_type=jnp.float32)
+    parts = lax.all_gather(block, "mp", axis=0, tiled=False)
+    attended = parts.sum(axis=0)
     hidden_state = inputs_f + attended.reshape(count, length_half, width)
     normed_second = (
         normalize(hidden_state, gain_second).astype(jnp.bfloat16).reshape(total_rows, width)

time: 1790 us -> 2100 us (1.17)
  waiting for transfers between devices: 1300 us -> 1590 us
    all_gather x0 -> x1, waiting for transfers between devices: none -> 626 us  [local(): parts = lax.all_gather(block, 'mp', axis=0, tiled=False)]
    psum x1 -> x0, waiting for transfers between devices: 320 us -> none  [local(): lax.psum(jnp.dot(mixed_flat, out_full, preferred_element_type=jnp.float32...]
  transfers between devices with their start and end apart: 23 -> 23, of which waited for: 17 -> 17; matrix products, arithmetic and copies ran while one was open for 15% -> 14% of each run, Pallas kernels for 0% -> 0%
where the time goes in v1:
time: 2100 us; the launch traced here: 2090 us
  waiting for transfers between devices  1590 us (76%)
  local copies, waits for them, and re-layouts  144 us (7%)
  matrix products  128 us (6%)
  other arithmetic  106 us (5%)
  blocking collectives  75.8 us (4%)
  loops' own time  21.7 us (1%)
    all_gather x1, waiting for transfers between devices, local(): parts = lax.all_gather(block, 'mp', axis=0, tiled=False)  626 us
    reduce_scatter x1, waiting for transfers between devices, local(): lax.psum_scatter(grad_second_part, 'mp', scatter_dimension=1, tiled=True)  204 us
    reduce_scatter x1, waiting for transfers between devices, local(): lax.psum_scatter(ffn_part.reshape(count, length_half, width), 'mp', scatt...  118 us
    reduce_scatter x1, waiting for transfers between devices, local(): lax.psum_scatter(grad_up_sum, ('dp', 'ctx'), scatter_dimension=0, tiled=T...  92 us
    all_gather x1, waiting for transfers between devices, local(): lax.all_gather(inputs, 'mp', axis=1, tiled=True)  88.5 us
    unnamed x4, blocking collectives  75.8 us
    all_gather x1, waiting for transfers between devices, local(): lax.all_gather(grad_hidden_shard.astype(jnp.bfloat16), 'mp', axis=1, tile...  64.2 us
    all_gather x1, waiting for transfers between devices, local(): lax.all_gather(cotangent, 'mp', axis=1, tiled=True)  52.7 us
  transfers between devices with their start and end apart: 23, of which 17 were waited for; matrix products, arithmetic and copies ran while one was open for 14% of the time, Pallas kernels for 0%

profile of v1, /device:TPU:0, one launch (start us, length us, event | category | flops | bytes accessed | tf_op | source)
XLA Modules:
  0.0 2089.8 jit_solution(15448360332707482137)
XLA Ops:
  13.8 15.5 all-reduce.13
  38.4 24.4 %all-gather.16.cloned.1.call-done = bf16[1536,384]{1,0:T(8,128)(2,1)} async-done(((bf16[192,384]{1,0:T(8,128)(2,1)}), bf16[1536,384]{1,0:T(8,128)(2,1)}) %all-gather.16.cloned.1.call-update) | async-done | bytes 1179664 | tf_op jit(solution)/shard_map/all_gather | solution.py:56
  64.4 24.4 %all-gather.14.cloned.1.call-done = bf16[1536,384]{1,0:T(8,128)(2,1)} async-done(((bf16[192,384]{1,0:T(8,128)(2,1)}), bf16[1536,384]{1,0:T(8,128)(2,1)}) %all-gather.14.cloned.1.call-update) | async-done | bytes 1179664 | tf_op jit(solution)/shard_map/all_gather | solution.py:58
  91.2 88.5 %all-gather.12.cloned.1.call-done = bf16[3,512,1536]{2,1,0:T(8,128)(2,1)} async-done(((bf16[3,128,1536]{2,1,0:T(8,128)(2,1)}), bf16[3,512,1536]{2,1,0:T(8,128)(2,1)}) %all-gather.12.cloned.1.call-update) | async-done | bytes 4718608 | tf_op jit(solution)/shard_map/all_gather | solution.py:68
  207.5 42.9 %while.32 = (s32[]{:T(128)}, bf16[3,512,3,128]{1,3,2,0:T(8,128)(2,1)}, f32[3,3,512]{2,1,0:T(4,128)}, bf16[3,512,3,128]{3,1,2,0:T(8,128)(2,1)}, bf16[3,512,3,128]...) while((s32[]{:T(128)}, ...), condition=%wide.region_4.5_spmd.clone, body=%wide.region_1.4_spmd.clone.sunk | while | flops 828570112 | bytes 53273240 | solution.py:123
  254.2 8.1 fusion.133
  266.4 626.4 %all-gather.30.cloned.1.call-done = f32[6144,1536]{1,0:T(8,128)} async-done(((f32[1536,1536]{1,0:T(8,128)}), f32[6144,1536]{1,0:T(8,128)}) %all-gather.30.cloned.1.call-update) | async-done | bytes 37748752 | tf_op jit(solution)/shard_map/all_gather | solution.py:128
  892.8 19.6 reduce_sum.108
  912.4 9.9 multiply_reduce_fusion.2
  929.6 52.7 %all-gather.26.cloned.1.call-done = bf16[3,512,1536]{2,1,0:T(8,128)(2,1)} async-done(((bf16[3,128,1536]{2,1,0:T(8,128)(2,1)}), bf16[3,512,1536]{2,1,0:T(8,128)(2,1)}) %all-gather.26.cloned.1.call-update) | async-done | bytes 4718608 | tf_op jit(solution)/shard_map/all_gather | solution.py:69
  982.4 46.5 %all-gather.24.cloned.1.call-done = bf16[8,192,1536]{1,0,2:T(8,128)(2,1)} async-done(((bf16[8,192,192]{1,0,2:T(8,128)(2,1)}), bf16[8,192,1536]{1,0,2:T(8,128)(2,1)}) %all-gather.24.cloned.1.call-update) | async-done | bytes 4718608 | tf_op jit(solution)/shard_map/all_gather | solution.py:61
  1028.8 47.4 %all-gather.22.cloned.1.call-done = bf16[1536,8,192]{2,1,0:T(8,128)(2,1)} async-done(((bf16[192,8,192]{2,1,0:T(8,128)(2,1)}), bf16[1536,8,192]{2,1,0:T(8,128)(2,1)}) %all-gather.22.cloned.1.call-update) | async-done | bytes 4718608 | tf_op jit(solution)/shard_map/all_gather | solution.py:60
  1076.3 72.0 %conditional.1 = (f32[1536,1536]{1,0:T(8,128)}, f32[1536,1536]{1,0:T(8,128)}, f32[1536,8,192]{0,2,1:T(8,128)}, f32[8,192,1536]{2,1,0:T(8,128)}) conditional(s32[]{:T(128)} %clamp.3, (bf16[1536,8,192]{2,1,0:T(8,128)(2,1)}, bf16[1536,1536]{1,0:T(8,128)(2,1)}, bf16[8,192,1536]{1,0,2:T(8,128)(2,1)}, ...), branch_computations={%region_7.8_spmd, %region_8.9_spmd, %region_9.10_spmd, %region_10.... | conditional | flops 43576197120 | bytes 273678624 | solution.py:171
  1076.4 8.8 copy.70
  1089.4 8.8 copy.71
  1148.4 204.1 %reduce-scatter.14.cloned.1.call-done = f32[3,128,1536]{2,1,0:T(8,128)} async-done(((f32[3,512,1536]{2,1,0:T(8,128)}), f32[3,128,1536]{2,1,0:T(8,128)}) %reduce-scatter.14.cloned.1.call-update) | async-done | bytes 2359312 | tf_op jit(solution)/shard_map/reduce_scatter | solution.py:180
  1359.7 12.9 copy.90
  1372.6 13.1 reshape.344
  1385.8 64.2 %all-gather.28.cloned.1.call-done = bf16[3,512,1536]{2,1,0:T(8,128)(2,1)} async-done(((bf16[3,128,1536]{2,1,0:T(8,128)(2,1)}), bf16[3,512,1536]{2,1,0:T(8,128)(2,1)}) %all-gather.28.cloned.1.call-update) | async-done | bytes 4718608 | tf_op jit(solution)/shard_map/all_gather | solution.py:194
  1458.6 52.4 %while.33 = (s32[]{:T(128)}, f32[3,512,3,128]{1,3,2,0:T(8,128)}, f32[3,512,3,128]{1,3,2,0:T(8,128)}, bf16[3,512,3,128]{1,3,2,0:T(8,128)(2,1)}, f32[3,512,3,128]{...) while((s32[]{:T(128)}, f32[3,512,3,128]{1,3,2,0:T(8,128)}, ...), condition=%wide.region_18.19_spmd.clone, body=%wide.region_16.18_spmd.clone.sunk | while | flops 2043214336 | bytes 65065664 | solution.py:238
  1551.5 12.9 copy.85
  1564.9 6.9 fusion.131
  1594.7 7.4 multiply_reduce_fusion.1
  1602.1 19.0 all-reduce.10
  1633.2 17.3 all-reduce.8
  1652.6 23.9 %all-reduce.12 = (f32[1536]{0:T(1024)}, f32[1536]{0:T(1024)}) all-reduce(f32[1536]{0:T(1024)} %fusion.144, f32[1536]{0:T(1024)} %dynamic-slice_reduce_fusion), channel_id=13, replica_groups=mesh['dp'=4,'ctx'=2,'mp'=4] {'dp','ctx'}, use_global_device_ids=true, to_apply=%region_29.30.clone | all-reduce | flops 3072 | bytes 24576
  1682.3 117.6 %reduce-scatter.12.cloned.1.call-done = f32[3,128,1536]{2,1,0:T(8,128)} async-done(((f32[3,512,1536]{2,1,0:T(8,128)}), f32[3,128,1536]{2,1,0:T(8,128)}) %reduce-scatter.12.cloned.1.call-update) | async-done | bytes 2359312 | tf_op jit(solution)/shard_map/reduce_scatter | solution.py:177
  1805.0 92.0 %reduce-scatter.26.cloned.1.call-done = f32[192,8,192]{2,1,0:T(8,128)} async-done(((f32[1536,8,192]{2,1,0:T(8,128)}), f32[192,8,192]{2,1,0:T(8,128)}) %reduce-scatter.26.cloned.1.call-update) | async-done | bytes 1179664 | tf_op jit(solution)/shard_map/reduce_scatter | solution.py:305
  1897.0 46.3 %reduce-scatter.24.cloned.1.call-done = f32[384,192]{0,1:T(8,128)} async-done(((f32[384,1536]{0,1:T(8,128)}), f32[384,192]{0,1:T(8,128)}) %reduce-scatter.24.cloned.1.call-update) | async-done | bytes 294928 | tf_op jit(solution)/shard_map/reduce_scatter | solution.py:304
  1943.3 46.6 %reduce-scatter.22.cloned.1.call-done = f32[192,384]{1,0:T(8,128)} async-done(((f32[1536,384]{1,0:T(8,128)}), f32[192,384]{1,0:T(8,128)}) %reduce-scatter.22.cloned.1.call-update) | async-done | bytes 294928 | tf_op jit(solution)/shard_map/reduce_scatter | solution.py:303
  1990.0 46.3 %reduce-scatter.20.cloned.1.call-done = f32[192,384]{1,0:T(8,128)} async-done(((f32[1536,384]{1,0:T(8,128)}), f32[192,384]{1,0:T(8,128)}) %reduce-scatter.20.cloned.1.call-update) | async-done | bytes 294928 | tf_op jit(solution)/shard_map/reduce_scatter | solution.py:302
  2036.3 46.8 %reduce-scatter.18.cloned.1.call-done = f32[192,384]{1,0:T(8,128)} async-done(((f32[1536,384]{1,0:T(8,128)}), f32[192,384]{1,0:T(8,128)}) %reduce-scatter.18.cloned.1.call-update) | async-done | bytes 294928 | tf_op jit(solution)/shard_map/reduce_scatter | solution.py:301
  (286 shorter events, 293.3 us)
Async XLA Ops:
  7.2 29.7 %all-gather.18.cloned.1.call-start = ((), (), s32[]{:S(2)}) async-start(), calls=%async_computation.12 | async-start | bytes 1327104 | tf_op jit(solution)/shard_map/all_gather | solution.py:57
  7.9 54.9 %all-gather.16.cloned.1.call-start = ((), (), s32[]{:S(2)}) async-start(), calls=%async_computation.11 | async-start | bytes 1327104 | tf_op jit(solution)/shard_map/all_gather | solution.py:56
  8.7 80.2 %all-gather.14.cloned.1.call-start = ((), (), s32[]{:S(2)}) async-start(), calls=%async_computation.10 | async-start | bytes 1327104 | tf_op jit(solution)/shard_map/all_gather | solution.py:58
  9.4 170.3 %all-gather.12.cloned.1.call-start = ((), (), s32[]{:S(2)}) async-start(), calls=%async_computation.9 | async-start | bytes 5898240 | tf_op jit(solution)/shard_map/all_gather | solution.py:68
  10.0 244.3 %all-gather.20.cloned.1.call-start = ((), (), s32[]{:S(2)}) async-start(), calls=%async_computation.13 | async-start | bytes 1327104 | tf_op jit(solution)/shard_map/all_gather | solution.py:59
  29.3 153.9 %copy-start.25 = (f32[1536]{0:T(1024)}, f32[1536]{0:T(1024)S(1)}, u32[]{:S(2)}) copy-start(f32[1536]{0:T(1024)S(1)} %convert_element_type.148) | copy-start | bytes 18436
  30.5 158.1 %copy-start.14 = (f32[512,64]{0,1:T(8,128)}, f32[512,64]{0,1:T(8,128)S(1)}, u32[]{:S(2)}) copy-start(f32[512,64]{0,1:T(8,128)S(1)} %get-tuple-element.456) | copy-start | bytes 393220
  190.4 14.7 collective-permute-start.1
  197.0 10.5 collective-permute-start
  199.4 693.4 %all-gather.30.cloned.1.call-start = ((), (), s32[]{:S(2)}) async-start(), calls=%async_computation.26 | async-start | bytes 47185920 | tf_op jit(solution)/shard_map/all_gather | solution.py:128
  262.4 720.0 %all-gather.26.cloned.1.call-start = ((), (), s32[]{:S(2)}) async-start(), calls=%async_computation.16 | async-start | bytes 5898240 | tf_op jit(solution)/shard_map/all_gather | solution.py:69
  263.1 765.7 %all-gather.24.cloned.1.call-start = ((), (), s32[]{:S(2)}) async-start(), calls=%async_computation.15 | async-start | bytes 7077888 | tf_op jit(solution)/shard_map/all_gather | solution.py:61
  265.0 811.3 %all-gather.22.cloned.1.call-start = ((), (), s32[]{:S(2)}) async-start(), calls=%async_computation.14 | async-start | bytes 7077888 | tf_op jit(solution)/shard_map/all_gather | solution.py:60
  265.7 1086.8 %reduce-scatter.14.cloned.1.call-start = ((), (), s32[]{:S(2)}) async-start(), calls=%async_computation.18 | async-start | bytes 11796480 | tf_op jit(solution)/shard_map/reduce_scatter | solution.py:180
  266.3 656.0 %copy-start.22 = (f32[1536]{0:T(1024)}, f32[1536]{0:T(1024)S(1)}, u32[]{:S(2)}) copy-start(f32[1536]{0:T(1024)S(1)} %convert_element_type.152) | copy-start | bytes 18436
  1148.3 204.2 %copy-start.23 = (f32[1536]{0:T(1024)S(1)}, f32[1536]{0:T(1024)}, u32[]{:S(2)}) copy-start(f32[1536]{0:T(1024)} %copy-done.22) | copy-start | bytes 18436
  1148.4 301.6 %all-gather.28.cloned.1.call-start = ((), (), s32[]{:S(2)}) async-start(), calls=%async_computation.19 | async-start | bytes 5898240 | tf_op jit(solution)/shard_map/all_gather | solution.py:194
  1148.4 207.8 %copy-start.8 = (bf16[3,128,1536]{2,1,0:T(8,128)(2,1)S(1)}, bf16[3,128,1536]{2,1,0:T(8,128)(2,1)}, u32[]{:S(2)}) copy-start(bf16[3,128,1536]{2,1,0:T(8,128)(2,1)} %param.27) | copy-start | bytes 3538948
  1359.6 262.8 %reduce-scatter.28.cloned.1.call-start = ((), (), s32[]{:S(2)}) async-start(), calls=%async_computation.27 | async-start | bytes 10616832
  1385.7 64.3 %copy-start.16 = (bf16[384,1536]{0,1:T(8,128)(2,1)S(1)}, bf16[384,1536]{0,1:T(8,128)(2,1)}, u32[]{:S(2)}) copy-start(bf16[384,1536]{0,1:T(8,128)(2,1)} %all-gather.20.cloned.1.call-done) | copy-start | bytes 3538948
  1385.7 293.4 %reduce-scatter.16.cloned.1.call-start = ((), (), s32[]{:S(2)}) async-start(), calls=%async_computation.20 | async-start | bytes 5898240 | tf_op jit(solution)/shard_map/reduce_scatter | solution.py:278
  1511.0 4.7 collective-permute-start.3
  1512.3 6.6 collective-permute-start.2
  1550.9 249.0 %reduce-scatter.12.cloned.1.call-start = ((), (), s32[]{:S(2)}) async-start(), calls=%async_computation.17 | async-start | bytes 11796480 | tf_op jit(solution)/shard_map/reduce_scatter | solution.py:177
  1551.5 345.5 %reduce-scatter.26.cloned.1.call-start = ((), (), s32[]{:S(2)}) async-start(), calls=%async_computation.25 | async-start | bytes 14155776 | tf_op jit(solution)/shard_map/reduce_scatter | solution.py:305
  1564.5 378.9 %reduce-scatter.24.cloned.1.call-start = ((), (), s32[]{:S(2)}) async-start(), calls=%async_computation.24 | async-start | bytes 2654208 | tf_op jit(solution)/shard_map/reduce_scatter | solution.py:304
  1571.9 418.1 %reduce-scatter.22.cloned.1.call-start = ((), (), s32[]{:S(2)}) async-start(), calls=%async_computation.23 | async-start | bytes 2654208 | tf_op jit(solution)/shard_map/reduce_scatter | solution.py:303
  1578.4 457.9 %reduce-scatter.20.cloned.1.call-start = ((), (), s32[]{:S(2)}) async-start(), calls=%async_computation.22 | async-start | bytes 2654208 | tf_op jit(solution)/shard_map/reduce_scatter | solution.py:302
  1584.9 498.2 %reduce-scatter.18.cloned.1.call-start = ((), (), s32[]{:S(2)}) async-start(), calls=%async_computation.21 | async-start | bytes 2654208 | tf_op jit(solution)/shard_map/reduce_scatter | solution.py:301
  1626.1 53.1 %copy-start.26 = (f32[1536]{0:T(1024)S(1)}, f32[1536]{0:T(1024)}, u32[]{:S(2)}) copy-start(f32[1536]{0:T(1024)} %copy-done.25) | copy-start | bytes 18436
  1632.6 167.3 %copy-start.6 = (f32[3,128,1536]{2,1,0:T(8,128)S(1)}, f32[3,128,1536]{2,1,0:T(8,128)}, u32[]{:S(2)}) copy-start(f32[3,128,1536]{2,1,0:T(8,128)} %reduce-scatter.14.cloned.1.call-done) | copy-start | bytes 7077892
  1632.6 167.2 %copy-start.24 = (f32[1536]{0:T(1024)S(1)}, f32[1536]{0:T(1024)}, u32[]{:S(2)}) copy-start(f32[1536]{0:T(1024)} %copy-done.22) | copy-start | bytes 18436
  (33 other events, 202.8 us)
Sparse Core Ops, SparseCore 0:
  9.9 26.9 all-gather.17
  38.8 24.0 all-gather.15
  64.7 24.0 all-gather.13
  90.3 89.3 all-gather.11
  199.5 22.5 all-gather.19
  262.5 630.2 all-gather.29
  894.4 87.9 all-gather.25
  984.8 43.9 all-gather.23
  1030.7 45.5 all-gather.21
  1148.5 204.0 reduce-scatter.13
  1359.7 90.2 all-gather.27
  1453.3 74.9 reduce-scatter.27
  1551.0 84.7 reduce-scatter.15
  1638.0 161.8 reduce-scatter.11
  1803.8 93.1 reduce-scatter.25
  1900.8 42.4 reduce-scatter.23
  1947.5 42.4 reduce-scatter.21
  1993.7 42.4 reduce-scatter.19
  2040.6 42.4 reduce-scatter.17
